TPU v7x, 256 devices: a whole 4x4x8 slice. The times are simulated.
256 devices in a mesh: seq: 32 (over x, z), tp: 8 (over y, core).
Axes of the slice: x: 4, y: 4, z: 8, core: 2. Of those that a mesh axis runs over, the one named last changes fastest.
Arguments:
- event_vectors: bfloat16 [16384, 6144], P('seq'), may hold values from -6 to 6
- question_projector: bfloat16 [6144, 4096], P('seq', 'tp'), may hold values from -0.078125 to 0.078125
- lookup_projector: bfloat16 [6144, 4096], P('seq', 'tp'), may hold values from -0.078125 to 0.078125
- content_projector: bfloat16 [6144, 4096], P('seq', 'tp'), may hold values from -0.078125 to 0.078125
- channel_fading_speed: float32 [32], P('tp'), may hold values from 1.2207031e-05 to 0.03334
- surge_fading: float32 [16384], P('seq'), may hold values from -0.6932 to 0, as said below
- channel_scaling_coefficient: float32 [4096], P('tp'), may hold values from 0.1 to 1.9
- final_projector: bfloat16 [4096, 6144], P('seq', 'tp'), may hold values from -0.09375 to 0.09375
Outputs:
- mixed: bfloat16 [16384, 6144], P('seq', 'tp')
Inputs may be any that keep to these rules, and one draw needn't show every extreme that they name: `surge_fading`: zero at all but a few positions of the sequence.
All inputs are finite; a program needn't handle non-finite values.
Results may differ from a plain program's by a relative error of at most 0.0063.
Values may be sent and summed in bfloat16 or wider, within the bound.
A program may use at most 128 MiB of HBM per device.

v0:
```python
import jax
import jax.numpy as jnp
from jax import lax
from jax.sharding import PartitionSpec as P

HD = 128
SPAN_LENGTH = 512


def entering(part, axis, combine, identity):
    place = lax.axis_index(axis)
    gathered = jax.tree.map(lambda a: lax.all_gather(a, axis), part)
    state = jax.tree.map(lambda a, e: jnp.zeros_like(a) + jnp.asarray(e, a.dtype), part, identity)

    def one(step, state):
        return combine(
            state, jax.tree.map(lambda a: lax.dynamic_index_in_dim(a, step, 0, False), gathered)
        )

    return lax.fori_loop(0, place, one, state)


def block_pass(carry, inputs):
    carried, before = carry
    query_block, key_block, value_block, log_block = inputs
    inside = jnp.cumsum(log_block, axis=0)
    block_total = inside[-1]
    highest = lax.Precision.HIGHEST
    scores = jnp.einsum("thd,shd->hts", query_block, key_block, precision=highest)
    spread_log = inside.T[:, :, None] - inside.T[:, None, :]
    rows_index = lax.broadcasted_iota(jnp.int32, (SPAN_LENGTH, SPAN_LENGTH), 0)
    cols_index = lax.broadcasted_iota(jnp.int32, (SPAN_LENGTH, SPAN_LENGTH), 1)
    causal = (rows_index >= cols_index)[None, :, :]
    weight = jnp.where(causal, jnp.exp(jnp.where(causal, spread_log, 0.0)), 0.0)
    within = jnp.einsum("hts,shd->thd", scores * weight, value_block, precision=highest)
    across = jnp.einsum(
        "thd,hde->the", query_block * jnp.exp(inside)[:, :, None], carried, precision=highest
    )
    updated = jnp.exp(block_total)[:, None, None] * carried + jnp.einsum(
        "shd,she->hde",
        key_block * jnp.exp(block_total[None, :] - inside)[:, :, None],
        value_block,
        precision=highest,
    )
    factor = jnp.exp(before[None, :] + inside)
    return ((updated, before + block_total), (within + across, factor))


def chain_combine(earlier, later):
    return (earlier[0] + later[0], jnp.exp(later[0])[:, None, None] * earlier[1] + later[1])


def local(
    event_vectors,
    question_projector,
    lookup_projector,
    content_projector,
    channel_fading_speed,
    surge_fading,
    channel_scaling_coefficient,
    final_projector,
):
    tok_count = event_vectors.shape[0]
    number_of_heads = channel_fading_speed.shape[0]

    def project_rows(shard_rows):
        return jnp.dot(event_vectors, shard_rows, preferred_element_type=jnp.float32)

    query_sum = project_rows(lax.all_gather(question_projector, "seq", axis=0, tiled=True))
    key_sum = project_rows(lax.all_gather(lookup_projector, "seq", axis=0, tiled=True))
    value_sum = project_rows(lax.all_gather(content_projector, "seq", axis=0, tiled=True))
    queries = jax.nn.silu(query_sum).astype(jnp.bfloat16)
    keys_act = jax.nn.silu(key_sum).astype(jnp.bfloat16)
    values_act = value_sum.astype(jnp.bfloat16)
    span_count = tok_count // SPAN_LENGTH
    shaped = (span_count, SPAN_LENGTH, number_of_heads, HD)
    query_blocks = queries.astype(jnp.float32).reshape(shaped)
    key_blocks = keys_act.astype(jnp.float32).reshape(shaped)
    value_blocks = values_act.astype(jnp.float32).reshape(shaped)
    stepwise_fading_exponent = (surge_fading[:, None] - channel_fading_speed[None, :]).reshape(
        (span_count, SPAN_LENGTH, number_of_heads)
    )
    start = (
        jnp.zeros((number_of_heads, HD, HD), jnp.float32),
        jnp.zeros((number_of_heads,), jnp.float32),
    )
    (local_state, local_log), (outputs, factors) = lax.scan(
        block_pass, start, (query_blocks, key_blocks, value_blocks, stepwise_fading_exponent)
    )
    identity = (
        jnp.zeros((number_of_heads,), jnp.float32),
        jnp.zeros((number_of_heads, HD, HD), jnp.float32),
    )
    prior_log, incoming = entering((local_log, local_state), "seq", chain_combine, identity)
    query_flat = query_blocks.reshape((tok_count, number_of_heads, HD))
    reached = jnp.einsum("thd,hde->the", query_flat, incoming, precision=lax.Precision.HIGHEST)
    attention = (
        outputs.reshape((tok_count, number_of_heads, HD))
        + factors.reshape((tok_count, number_of_heads))[:, :, None] * reached
    )
    meansq = jnp.mean(attention * attention, axis=-1, keepdims=True)
    normed = (
        attention
        / jnp.sqrt(meansq + 1e-05)
        * channel_scaling_coefficient.reshape((number_of_heads, HD))[None, :, :]
    )
    normed = normed.reshape((tok_count, number_of_heads * HD)).astype(jnp.bfloat16)
    every_head = lax.all_gather(normed, "tp", axis=1, tiled=True)
    mixed = jnp.dot(
        every_head,
        lax.all_gather(final_projector, "seq", axis=0, tiled=True),
        preferred_element_type=jnp.float32,
    )
    return mixed.astype(jnp.bfloat16)


def solution(mesh):
    in_specs = (
        P("seq", None),
        P("seq", "tp"),
        P("seq", "tp"),
        P("seq", "tp"),
        P("tp"),
        P("seq"),
        P("tp"),
        P("seq", "tp"),
    )
    out_specs = P("seq", "tp")
    return jax.shard_map(local, mesh=mesh, in_specs=in_specs, out_specs=out_specs, check_vma=False)
```

profile of v0, /device:TPU:1, one launch (start us, length us, event | category | flops | bytes accessed | tf_op | source)
XLA Modules:
  0.0 514.1 jit_solution(17631043664003188020)
XLA Ops:
  6.5 0.0 all-gather.9.cloned.1.call-start
  6.5 0.7 all-gather.9.cloned.1.call-update
  7.3 0.0 all-gather.13.cloned.1.call-start
  7.3 0.7 all-gather.13.cloned.1.call-update
  8.0 0.0 all-gather.11.cloned.1.call-start
  8.1 0.7 all-gather.11.cloned.1.call-update
  8.7 0.0 all-gather.19.cloned.1.call-start
  8.8 0.8 broadcast_subtract_fusion
  9.6 1.2 reduce-window.6
  10.8 0.2 slice_reduce_fusion
  10.9 0.2 reduce-window.9
  11.1 0.1 add_bitcast_fusion
  11.2 0.2 slice_reduce_fusion.1
  11.4 0.1 subtract_exponential_fusion
  11.5 90.6 %all-gather.9.cloned.1.call-done = bf16[6144,512]{1,0:T(8,128)(2,1)} async-done(((bf16[192,512]{1,0:T(8,128)(2,1)}), bf16[6144,512]{1,0:T(8,128)(2,1)}) %all-gather.9.cloned.1.call-update) | async-done | bytes 6291472 | tf_op jit(solution)/shard_map/all_gather | solution.py:71
  102.1 8.1 %convolution_convert_fusion.1 = bf16[512,512]{0,1:T(8,128)(2,1)S(1)} fusion(bf16[512,6144]{1,0:T(8,128)(2,1)} %param.10, bf16[6144,512]{1,0:T(8,128)(2,1)} %all-gather.9.cloned.1.call-done), kind=kOutput, calls=%fused_computation.18 | convolution fusion | flops 3221487616 | bytes 13107200 | tf_op jit(solution)/shard_map/dot_general | solution.py:67
  110.2 80.2 %all-gather.13.cloned.1.call-done = bf16[6144,512]{1,0:T(8,128)(2,1)} async-done(((bf16[192,512]{1,0:T(8,128)(2,1)}), bf16[6144,512]{1,0:T(8,128)(2,1)}) %all-gather.13.cloned.1.call-update) | async-done | bytes 6291472 | tf_op jit(solution)/shard_map/all_gather | solution.py:70
  190.4 8.2 %multiply_convert_fusion.1 = bf16[512,512]{0,1:T(8,128)(2,1)S(1)} fusion(bf16[512,6144]{1,0:T(8,128)(2,1)} %param.10, bf16[6144,512]{1,0:T(8,128)(2,1)} %all-gather.13.cloned.1.call-done), kind=kOutput, calls=%fused_computation.27 | convolution fusion | flops 3222536192 | bytes 13107200 | tf_op jit(solution)/shard_map/dot_general | solution.py:67
  198.6 1.4 convolution_add_fusion.1
  199.9 0.0 all-gather.19.cloned.1.call-update
  200.0 0.0 all-gather.17.cloned.1.call-start
  200.0 0.5 all-gather.17.cloned.1.call-update
  200.6 0.0 all-gather.15.cloned.1.call-start
  200.6 31.6 %all-gather.1 = f32[32,1,4]{2,1,0:T(1,128)S(1)} all-gather(f32[1,1,4]{2,1,0:T(1,128)S(1)} %bitcast.69), channel_id=1, replica_groups=mesh['seq'=32,'tp'=8] {'seq'}, dimensions={0}, use_global_device_ids=true | all-gather | bytes 528 | tf_op jit(solution)/shard_map/all_gather | solution.py:12
  232.2 0.1 iota_compare_fusion
  232.3 46.4 %all-gather.11.cloned.1.call-done = bf16[6144,512]{1,0:T(8,128)(2,1)} async-done(((bf16[192,512]{1,0:T(8,128)(2,1)}), bf16[6144,512]{1,0:T(8,128)(2,1)}) %all-gather.11.cloned.1.call-update) | async-done | bytes 6291472 | tf_op jit(solution)/shard_map/all_gather | solution.py:69
  278.7 8.2 %multiply_convert_fusion.2 = bf16[512,512]{0,1:T(8,128)(2,1)S(1)} fusion(bf16[512,6144]{1,0:T(8,128)(2,1)} %param.10, bf16[6144,512]{1,0:T(8,128)(2,1)} %all-gather.11.cloned.1.call-done), kind=kOutput, calls=%fused_computation.28 | convolution fusion | flops 3222536192 | bytes 13107200 | tf_op jit(solution)/shard_map/dot_general | solution.py:67
  286.9 0.7 fusion.23
  287.6 3.7 fusion
  291.3 0.0 copy-start
  291.3 1.0 fusion.12
  292.4 84.0 %all-gather.19.cloned.1.call-done = f32[128,128,128]{2,1,0:T(8,128)} async-done(((f32[4,128,128]{2,1,0:T(8,128)}), f32[128,128,128]{2,1,0:T(8,128)}) %all-gather.19.cloned.1.call-update) | async-done | bytes 8388624 | tf_op jit(solution)/shard_map/all_gather | solution.py:12
  376.4 0.2 while.3
  376.6 0.7 multiply_reduce_fusion
  377.4 0.0 copy-done
  377.4 0.9 multiply_convert_fusion
  378.3 0.0 all-gather.15.cloned.1.call-update
  378.4 86.3 %all-gather.17.cloned.1.call-done = bf16[4096,768]{1,0:T(8,128)(2,1)} async-done(((bf16[128,768]{1,0:T(8,128)(2,1)}), bf16[4096,768]{1,0:T(8,128)(2,1)}) %all-gather.17.cloned.1.call-update) | async-done | bytes 6291472 | tf_op jit(solution)/shard_map/all_gather | solution.py:111
  464.6 34.2 %all-gather.15.cloned.1.call-done = bf16[512,4096]{0,1:T(8,128)(2,1)} async-done(((bf16[512,512]{0,1:T(8,128)(2,1)}), bf16[512,4096]{0,1:T(8,128)(2,1)}) %all-gather.15.cloned.1.call-update) | async-done | bytes 4194320 | tf_op jit(solution)/shard_map/all_gather | solution.py:108
  498.8 8.4 %convolution_convert_fusion = bf16[512,768]{1,0:T(8,128)(2,1)} fusion(bf16[512,4096]{0,1:T(8,128)(2,1)} %all-gather.15.cloned.1.call-done, bf16[4096,768]{1,0:T(8,128)(2,1)} %all-gather.17.cloned.1.call-done), kind=kOutput, calls=%fused_computation.12 | convolution fusion | flops 3221618688 | bytes 11272192 | tf_op jit(solution)/shard_map/dot_general | solution.py:109
  (4 shorter events, 0.0 us)
Async XLA Ops:
  6.5 95.6 %all-gather.9.cloned.1.call-start = ((), (), s32[]{:S(2)}) async-start(), calls=%async_computation | async-start | bytes 6488064 | tf_op jit(solution)/shard_map/all_gather | solution.py:71
  7.3 183.1 %all-gather.13.cloned.1.call-start = ((), (), s32[]{:S(2)}) async-start(), calls=%async_computation.2 | async-start | bytes 6488064 | tf_op jit(solution)/shard_map/all_gather | solution.py:70
  8.0 270.7 %all-gather.11.cloned.1.call-start = ((), (), s32[]{:S(2)}) async-start(), calls=%async_computation.1 | async-start | bytes 6488064 | tf_op jit(solution)/shard_map/all_gather | solution.py:69
  8.7 367.6 %all-gather.19.cloned.1.call-start = ((), (), s32[]{:S(2)}) async-start(), calls=%async_computation.5 | async-start | bytes 8650752 | tf_op jit(solution)/shard_map/all_gather | solution.py:12
  200.0 264.7 %all-gather.17.cloned.1.call-start = ((), (), s32[]{:S(2)}) async-start(), calls=%async_computation.4 | async-start | bytes 6488064 | tf_op jit(solution)/shard_map/all_gather | solution.py:111
  200.6 298.3 %all-gather.15.cloned.1.call-start = ((), (), s32[]{:S(2)}) async-start(), calls=%async_computation.3 | async-start | bytes 4718592 | tf_op jit(solution)/shard_map/all_gather | solution.py:108
  291.3 86.1 %copy-start = (f32[512]{0:T(512)S(1)}, f32[512]{0:T(512)}, u32[]{:S(2)}) copy-start(f32[512]{0:T(512)} %param.16) | copy-start | bytes 6148
Sparse Core Ops, SparseCore 0:
  9.9 92.1 all-gather.8
  104.7 85.6 all-gather.12
  192.9 85.6 all-gather.10
  281.1 95.1 all-gather.18
  378.8 85.8 all-gather.16
  466.3 32.4 all-gather.14
where the time goes:
time: 515 us; the launch traced here: 514 us
  waiting for transfers between devices  424 us (82%)
  matrix products  40.4 us (8%)
  blocking collectives  31.6 us (6%)
  between operations  13.6 us (3%)
    all_gather x1, waiting for transfers between devices, local(): lax.all_gather(content_projector, 'seq', axis=0, tiled=True)  90.6 us
    all_gather x1, waiting for transfers between devices, local(): lax.all_gather(final_projector, 'seq', axis=0, tiled=True)  86.3 us
    all_gather x1, waiting for transfers between devices, entering(): gathered = jax.tree.map(lambda a: lax.all_gather(a, axis), part)  84 us
    all_gather x1, waiting for transfers between devices, local(): lax.all_gather(lookup_projector, 'seq', axis=0, tiled=True)  80.2 us
    all_gather x1, waiting for transfers between devices, local(): lax.all_gather(question_projector, 'seq', axis=0, tiled=True)  46.4 us
    all_gather x1, waiting for transfers between devices, local(): every_head = lax.all_gather(normed, 'tp', axis=1, tiled=True)  34.2 us
    all_gather x1, blocking collectives, entering(): gathered = jax.tree.map(lambda a: lax.all_gather(a, axis), part)  31.6 us
    dot_general x3, matrix products, project_rows(): jnp.dot(event_vectors, shard_rows, preferred_element_type=jnp.float32)  24.4 us
  transfers between devices with their start and end apart: 6, of which 6 were waited for; matrix products, arithmetic and copies ran while one was open for 7% of the time, Pallas kernels for 0%

commit v1 on v0

v1 whole, which is shorter than its diff:
```python
import jax
import jax.numpy as jnp
from jax import lax
from jax.experimental import pallas as pl
from jax.experimental.pallas import tpu as pltpu
from jax.sharding import PartitionSpec as P

MESH = pl.DeviceIdType.MESH
F32 = jnp.float32
BF16 = jnp.bfloat16
NZ = 8
NY = 4
PIECES = 2
COPIES = 220


def aligned(value, by):
    return pl.multiple_of(value, by)


def kernel(
    x_hbm, wq_hbm, wk_hbm, wv_hbm, wo_hbm, aux_hbm, out_ref,
    xs, wk, wv, wq, wo, acc, part, kb, vb, qb, decay, aux,
    states, arrived, totals, tot_out, group_out, groups, prefix_out, prefix,
    normed, staged, oacc, ssem, rsem, lsem,
):
    s = lax.axis_index("seq")
    t = lax.axis_index("tp")
    x, z = s // NZ, s % NZ
    y, c = t // 2, t % 2
    region = x // 2
    is_home = 1 - (region + c) % 2
    xe = 3 - x
    xi = x + 1 - 2 * (x % 2)
    xt = is_home * x + (1 - is_home) * xe
    p = xt % 2
    home = is_home == 1
    away = is_home == 0

    def dev(cx, cy, cz, cc):
        return (cx * NZ + cz, cy * 2 + cc)

    z_dev = [dev(x, y, (z + d) % NZ, c) for d in range(NZ)]
    up, down = z_dev[1], z_dev[NZ - 1]
    inner = dev(xi, y, z, c)
    inner_other = dev(xi, y, z, 1 - c)
    across_chip = dev(xe, y, z, c)
    swap = dev(xe, y, z, 1 - c)
    other = dev(x, y, z, 1 - c)
    y_up = dev(x, (y + 1) % NY, z, c)
    y_down = dev(x, (y + 3) % NY, z, c)
    peers = z_dev[1:] + [inner, inner_other, across_chip, swap, other, y_up, y_down]

    used = [0]
    sent = []
    sent_away = []

    def remote(src, dst, device):
        i = used[0]
        used[0] += 1
        return pltpu.make_async_remote_copy(
            src_ref=src, dst_ref=dst, send_sem=ssem.at[i], recv_sem=rsem.at[i],
            device_id=device, device_id_type=MESH,
        )

    def send(src, dst, device):
        copy = remote(src, dst, device)
        copy.start()
        sent.append(copy)
        return copy

    barrier = pltpu.get_barrier_semaphore()
    for device in peers:
        pl.semaphore_signal(barrier, inc=1, device_id=device, device_id_type=MESH)
    pl.semaphore_wait(barrier, len(peers))

    own_row = aligned(192 * (p * NZ + z), 64)
    source_row = aligned(192 * ((x % 2) * NZ + z), 64)
    swaps = {}

    def own_piece(name, src, dst, index):
        local = pltpu.make_async_copy(src, dst, lsem.at[index])
        copy = remote(src, dst, swap)
        swaps[name] = (local, copy)

        @pl.when(home)
        def _():
            local.start()

        @pl.when(away)
        def _():
            copy.start()

        sent_away.append(copy)

    def wait_own(name):
        local, copy = swaps[name]

        @pl.when(home)
        def _():
            local.wait()

        @pl.when(away)
        def _():
            copy.wait_recv()

    own_piece("k", wk_hbm, wk.at[pl.ds(source_row, 192)], 0)
    own_piece("v", wv_hbm, wv.at[pl.ds(source_row, 192)], 1)
    own_piece("aux", aux_hbm, aux, 2)
    half_lane = aligned(3072 * c, 128)
    quarter = aligned(128 * y, 128)
    x_cross = send(
        x_hbm.at[pl.ds(quarter, 128), pl.ds(half_lane, 3072)],
        xs.at[region, pl.ds(quarter, 128)], across_chip,
    )
    own_piece("q", wq_hbm, wq.at[pl.ds(source_row, 192)], 3)
    x_local = pltpu.make_async_copy(x_hbm.at[:, pl.ds(half_lane, 3072)], xs.at[region], lsem.at[4])
    x_local.start()
    o_own_row = aligned(128 * s, 128)
    o_local = pltpu.make_async_copy(wo_hbm, wo.at[pl.ds(o_own_row, 128)], lsem.at[5])
    o_local.start()

    class Round:
        def __init__(self, own_x, nbr_x, own_z, hops):
            self.own_x, self.nbr_x, self.own_z = own_x, nbr_x, own_z
            self.parts = {"a": own_x, "b": nbr_x, "z": own_z}
            self.hops = hops
            self.ring = {}
            self.side = []

        def begin_flow(self, f):
            part = self.parts[f](z)
            self.ring[f, 0, 1] = send(part, part, up)
            self.ring[f, 1, 1] = send(part, part, down)

        def start(self):
            own = self.own_x(z)
            self.first = send(own, own, inner)
            self.begin_flow("a")
            self.begin_flow("z")
            own = self.own_z(z)
            self.side.append((0, send(own, own, inner)))

        def start_nbr(self):
            self.first.wait_recv()
            self.begin_flow("b")

        def step(self, d):
            for f in ("a", "z", "b"):
                for way in (0, 1):
                    limit = self.hops[f][way]
                    if d > limit:
                        continue
                    self.ring[f, way, d].wait_recv()
                    where = (z + NZ - d) % NZ if way == 0 else (z + d) % NZ
                    part = self.parts[f](where)
                    if d < limit:
                        self.ring[f, way, d + 1] = send(part, part, up if way == 0 else down)
                    if f == "z":
                        self.side.append((d, send(part, part, inner)))

        def wait_side(self, low, high):
            for d, copy in self.side:
                if low <= d <= high:
                    copy.wait_recv()

    def rows(ref, start, count, by):
        return ref.at[pl.ds(aligned(start, by), count)]

    kv = Round(
        lambda w: rows(wk, 192 * (p * NZ + w), 192, 64),
        lambda w: rows(wk, 192 * ((1 - p) * NZ + w), 192, 64),
        lambda w: rows(wv, 192 * (p * NZ + w), 192, 64),
        {"a": (4, 3), "b": (3, 4), "z": (4, 3)},
    )
    qr = Round(
        lambda w: rows(wq, 192 * (p * NZ + w), 96, 32),
        lambda w: rows(wq, 192 * ((1 - p) * NZ + w), 96, 32),
        lambda w: rows(wq, 192 * (p * NZ + w) + 96, 96, 32),
        {"a": (4, 3), "b": (3, 4), "z": (3, 4)},
    )
    orr = Round(
        lambda w: rows(wo, 128 * (x * NZ + w), 128, 128),
        lambda w: rows(wo, 128 * (xi * NZ + w), 128, 128),
        lambda w: rows(wo, 128 * (xe * NZ + w), 128, 128),
        {"a": (4, 3), "b": (3, 4), "z": (3, 4)},
    )

    weights = {0: wk, 1: wv, 2: wq}
    last_pair = ((z + 4) % NZ) // 2

    def mm_chunk(which, pair):
        low = aligned(384 * pair, 128)
        high = aligned(1536 + 384 * pair, 128)
        for i in which:
            w = weights[i]
            wcat = jnp.concatenate([w[pl.ds(low, 384)], w[pl.ds(high, 384)]], axis=0)
            for j in (0, 1):
                xcat = jnp.concatenate([xs[j, :, pl.ds(low, 384)], xs[j, :, pl.ds(high, 384)]], axis=1)
                acc[i, j] += jnp.dot(xcat, wcat, preferred_element_type=F32)

    def mm_three(which):
        @pl.loop(0, 3)
        def _(m):
            mm_chunk(which, (last_pair + 1 + m) % 4)

    wait_own("k")
    wait_own("v")
    kv.start()
    acc[...] = jnp.zeros_like(acc)
    kv.start_nbr()
    x_local.wait()

    wait_own("aux")
    t_col = lax.broadcasted_iota(jnp.int32, (512, 128), 0)
    lane = lax.broadcasted_iota(jnp.int32, (512, 128), 1)
    cs = jnp.zeros((512, 1), F32)
    for b in range(4):
        surge = jnp.broadcast_to(aux[b : b + 1, :], (512, 128))
        cs += jnp.sum(jnp.where(lane + 128 * b <= t_col, surge, 0.0), axis=1, keepdims=True)
    cs_row = jnp.broadcast_to(cs, (512, 128)).T[0:1, :]
    total = cs[511:512, :]
    steps = lax.broadcasted_iota(jnp.int32, (512, 1), 0).astype(F32)
    t_idx = lax.broadcasted_iota(jnp.int32, (512, 512), 0)
    s_idx = lax.broadcasted_iota(jnp.int32, (512, 512), 1)
    causal = t_idx >= s_idx
    apart = (t_idx - s_idx).astype(F32)
    spread = jnp.broadcast_to(cs, (512, 512)) - jnp.broadcast_to(cs_row, (512, 512))
    for h in range(4):
        speed = aux[8 + h : 9 + h, 0:1]
        exponent = jnp.where(causal, spread - apart * speed, 0.0)
        decay[h] = jnp.where(causal, jnp.exp(exponent), 0.0)
    tot_out[...] = jnp.broadcast_to(total, (8, 128))
    totals[z] = jnp.broadcast_to(total, (8, 128))
    tot_copies = [send(tot_out, totals.at[z], z_dev[d]) for d in range(1, NZ)]

    kv.step(1)
    wait_own("q")

    x_cross.wait_recv()
    theirs = 1 - region

    def x_rows(cy, start, count):
        return xs.at[theirs, pl.ds(aligned(128 * cy + start, 64), count)]

    own_q = x_rows(y, 0, 128)
    x_up = send(own_q, own_q, y_up)
    x_down = send(own_q, own_q, y_down)
    kv.step(2)
    x_up.wait_recv()
    far = x_rows((y + 3) % NY, 0, 64)
    x_up2 = send(far, far, y_up)
    x_down.wait_recv()
    far = x_rows((y + 1) % NY, 64, 64)
    x_down2 = send(far, far, y_down)
    o_swap_dst = wo.at[pl.ds(o_own_row, 128)]
    o_swap = send(wo_hbm, o_swap_dst, across_chip)
    kv.step(3)
    qr.start()
    x_up2.wait_recv()
    x_down2.wait_recv()
    kv.wait_side(0, 3)
    qr.start_nbr()
    mm_three((0, 1))
    kv.step(4)
    qr.step(1)
    kv.wait_side(4, 4)
    mm_chunk((0, 1), last_pair)
    k_part = send(acc.at[0, 1 - c], part.at[0], other)
    v_part = send(acc.at[1, 1 - c], part.at[1], other)
    qr.step(2)

    k_part.wait_recv()
    v_part.wait_recv()
    ksum = acc[0, c] + part[0]
    kb[...] = (ksum * (1.0 / (1.0 + jnp.exp(-ksum)))).astype(BF16)
    vb[...] = (acc[1, c] + part[1]).astype(BF16)
    for h in range(4):
        speed = aux[8 + h : 9 + h, 0:1]
        remain = jnp.exp((total - cs) - (511.0 - steps) * speed)
        kd = (kb[:, 128 * h : 128 * h + 128].astype(F32) * remain).astype(BF16)
        state = lax.dot_general(
            kd, vb[:, 128 * h : 128 * h + 128], (((0,), (0,)), ((), ())),
            preferred_element_type=F32,
        ).astype(BF16)
        states[2 * h] = state[0:64]
        states[2 * h + 1] = state[64:128]
    arrived[z] = states[z]
    state_copies = [
        send(states.at[(z + d) % NZ], arrived.at[z], z_dev[d]) for d in range(1, NZ)
    ]
    qr.step(3)
    orr_ready = [False]
    o_local.wait()
    o_swap.wait_recv()
    orr.start()
    qr.wait_side(0, 3)
    for copy in state_copies + tot_copies:
        copy.wait_recv()
    slice_speed = aux[pl.ds(8 + z // 2, 1), 0:1]
    run = jnp.zeros((64, 128), F32)
    run_tot = jnp.zeros((1, 1), F32)
    before = []
    for w in range(NZ):
        before.append((run, run_tot))
        tot = totals[w, 0:1, 0:1]
        run = jnp.exp(tot - 512.0 * slice_speed) * run + arrived[w].astype(F32)
        run_tot = run_tot + tot
    group_out[0:64, :] = run
    group_out[64:72, :] = jnp.broadcast_to(run_tot, (8, 128))
    groups[xt] = group_out[...]
    group_copies = [send(group_out, groups.at[xt], d) for d in (other, inner, inner_other)]
    mm_three((2,))
    orr.start_nbr()
    for copy in group_copies:
        copy.wait_recv()
    carry = jnp.zeros((64, 128), F32)
    for g in range(4):
        tot = groups[g, 64:65, 0:1]
        later = jnp.exp(tot - 4096.0 * slice_speed) * carry + groups[g, 0:64, :]
        carry = jnp.where(jnp.full((64, 128), g, jnp.int32) < xt, later, carry)
    for w in range(NZ):
        run, run_tot = before[w]
        prefix_out[w] = (run + jnp.exp(run_tot - (512.0 * w) * slice_speed) * carry).astype(BF16)
    prefix[z] = prefix_out[z]
    prefix_copies = [
        send(prefix_out.at[(z + d) % NZ], prefix.at[z], z_dev[d]) for d in range(1, NZ)
    ]
    qr.step(4)
    qr.wait_side(4, 4)
    mm_chunk((2,), last_pair)
    q_part = send(acc.at[2, 1 - c], part.at[2], other)
    for copy in prefix_copies:
        copy.wait_recv()
    q_part.wait_recv()
    qsum = acc[2, c] + part[2]
    qb[...] = (qsum * (1.0 / (1.0 + jnp.exp(-qsum)))).astype(BF16)

    width = 512 // PIECES
    swap_t = y * 2 + 1 - c
    swap_copies = []
    for piece in range(PIECES):
        for h in range(piece * 4 // PIECES, (piece + 1) * 4 // PIECES):
            cut = slice(128 * h, 128 * h + 128)
            speed = aux[8 + h : 9 + h, 0:1]
            q_h, k_h, v_h = qb[:, cut], kb[:, cut], vb[:, cut]
            scores = lax.dot_general(q_h, k_h, (((1,), (1,)), ((), ())), preferred_element_type=F32)
            inside = jnp.dot((scores * decay[h]).astype(BF16), v_h, preferred_element_type=F32)
            carried = prefix[2 * h : 2 * h + 2].reshape(128, 128)
            reach = jnp.exp(cs - (steps + 1.0) * speed)
            att = inside + reach * jnp.dot(q_h, carried, preferred_element_type=F32)
            square = jnp.mean(att * att, axis=1, keepdims=True)
            value = (att * lax.rsqrt(square + 1e-05) * aux[4 + h : 5 + h, :]).astype(BF16)

            @pl.when(home)
            def _():
                normed[t, :, cut] = value

            @pl.when(away)
            def _():
                staged[:, cut] = value

        lanes = pl.ds(piece * width, width)
        copy = remote(staged.at[:, lanes], normed.at[swap_t, :, lanes], swap)

        @pl.when(away)
        def _():
            copy.start()

        sent_away.append(copy)
        swap_copies.append(copy)

    orr.step(1)

    def block(cy, start, count, piece):
        return normed.at[cy * 2 + c, pl.ds(start, count), pl.ds(piece * width, width)]

    ring_up, ring_down, relays = [], [], []
    for piece in range(PIECES):
        copy = swap_copies[piece]

        @pl.when(away)
        def _():
            copy.wait_recv()

        mine = block(y, 0, 512, piece)
        ring_up.append(send(mine, mine, y_up))
        ring_down.append(send(mine, mine, y_down))
        relays.append(send(mine, mine, other))
    orr.step(2)
    ring_up2, ring_down2 = [], []
    for piece in range(PIECES):
        ring_up[piece].wait_recv()
        far = block((y + 3) % NY, 0, 256, piece)
        ring_up2.append(send(far, far, y_up))
        whole = block((y + 3) % NY, 0, 512, piece)
        relays.append(send(whole, whole, other))
        ring_down[piece].wait_recv()
        far = block((y + 1) % NY, 256, 256, piece)
        ring_down2.append(send(far, far, y_down))
        whole = block((y + 1) % NY, 0, 512, piece)
        relays.append(send(whole, whole, other))
    oacc[...] = jnp.zeros_like(oacc)
    orr.step(3)
    for piece in range(PIECES):
        ring_up2[piece].wait_recv()
        far = block((y + 2) % NY, 0, 256, piece)
        relays.append(send(far, far, other))
        ring_down2[piece].wait_recv()
        far = block((y + 2) % NY, 256, 256, piece)
        relays.append(send(far, far, other))
    orr.wait_side(0, 3)
    for copy in relays:
        copy.wait_recv()

    def out_chunk(pair):
        lanes = pl.ds(aligned(256 * (pair % 2), 128), 256)
        left = jnp.concatenate([normed[2 * g + pair // 2, :, lanes] for g in range(4)], axis=1)
        right = jnp.concatenate(
            [wo[pl.ds(aligned(1024 * g + 256 * pair, 256), 256)] for g in range(4)], axis=0
        )
        return jnp.dot(left, right, preferred_element_type=F32)

    @pl.loop(0, 3)
    def _(m):
        oacc[...] += out_chunk((last_pair + 1 + m) % 4)

    orr.step(4)
    orr.wait_side(4, 4)
    out_ref[...] = (oacc[...] + out_chunk(last_pair)).astype(BF16)

    for copy in sent:
        copy.wait_send()

    @pl.when(away)
    def _():
        for copy in sent_away:
            copy.wait_send()


def local(
    event_vectors,
    question_projector,
    lookup_projector,
    content_projector,
    channel_fading_speed,
    surge_fading,
    channel_scaling_coefficient,
    final_projector,
):
    aux = jnp.concatenate(
        [
            surge_fading.reshape(4, 128),
            channel_scaling_coefficient.reshape(4, 128),
            jnp.broadcast_to(channel_fading_speed[:, None], (4, 128)),
            jnp.zeros((4, 128), F32),
        ],
        axis=0,
    )
    return pl.pallas_call(
        kernel,
        out_shape=jax.ShapeDtypeStruct((512, 768), BF16),
        in_specs=[pl.BlockSpec(memory_space=pl.ANY)] * 6,
        out_specs=pl.BlockSpec(memory_space=pltpu.VMEM),
        scratch_shapes=[
            pltpu.VMEM((2, 512, 3072), BF16),
            pltpu.VMEM((3072, 512), BF16),
            pltpu.VMEM((3072, 512), BF16),
            pltpu.VMEM((3072, 512), BF16),
            pltpu.VMEM((4096, 768), BF16),
            pltpu.VMEM((3, 2, 512, 512), F32),
            pltpu.VMEM((3, 512, 512), F32),
            pltpu.VMEM((512, 512), BF16),
            pltpu.VMEM((512, 512), BF16),
            pltpu.VMEM((512, 512), BF16),
            pltpu.VMEM((4, 512, 512), F32),
            pltpu.VMEM((16, 128), F32),
            pltpu.VMEM((8, 64, 128), BF16),
            pltpu.VMEM((8, 64, 128), BF16),
            pltpu.VMEM((8, 8, 128), F32),
            pltpu.VMEM((8, 128), F32),
            pltpu.VMEM((72, 128), F32),
            pltpu.VMEM((4, 72, 128), F32),
            pltpu.VMEM((8, 64, 128), BF16),
            pltpu.VMEM((8, 64, 128), BF16),
            pltpu.VMEM((8, 512, 512), BF16),
            pltpu.VMEM((512, 512), BF16),
            pltpu.VMEM((512, 768), F32),
            pltpu.SemaphoreType.DMA((COPIES,)),
            pltpu.SemaphoreType.DMA((COPIES,)),
            pltpu.SemaphoreType.DMA((8,)),
        ],
        compiler_params=pltpu.CompilerParams(
            collective_id=0, has_side_effects=True, vmem_limit_bytes=67043328
        ),
    )(
        event_vectors,
        question_projector,
        lookup_projector,
        content_projector,
        final_projector,
        aux,
    )


def solution(mesh):
    in_specs = (
        P("seq", None),
        P("seq", "tp"),
        P("seq", "tp"),
        P("seq", "tp"),
        P("tp"),
        P("seq"),
        P("tp"),
        P("seq", "tp"),
    )
    out_specs = P("seq", "tp")
    return jax.shard_map(local, mesh=mesh, in_specs=in_specs, out_specs=out_specs, check_vma=False)
```

time: 515 us -> 163 us (0.32)
  waiting for transfers between devices: 424 us -> 0 us
  Pallas kernels: 0 us -> 158 us
  matrix products: 40.4 us -> 0 us
  blocking collectives: 31.6 us -> 0 us
  between operations: 13.6 us -> 0.01 us
    all_gather x6 -> x0, waiting for transfers between devices: 422 us -> none  [the longest x1 90.6 us: local(): lax.all_gather(content_projector, 'seq', axis=0, tiled=True)]
    pallas_call x0 -> x1, Pallas kernels: none -> 158 us  [local(): pl.pallas_call(kernel, out_shape=jax.ShapeDtypeStruct((512, 768), BF16),...]
    dot_general x9 -> x0, matrix products: 40.4 us -> none  [the longest x3 24.4 us: project_rows(): jnp.dot(event_vectors, shard_rows, preferred_element_type=jnp.float32)]
    all_gather x1 -> x0, blocking collectives: 31.6 us -> none  [entering(): gathered = jax.tree.map(lambda a: lax.all_gather(a, axis), part)]
  transfers between devices with their start and end apart: 6 -> 0, of which waited for: 6 -> 0; matrix products, arithmetic and copies ran while one was open for 7% -> 0% of each run, Pallas kernels for 0% -> 0%
where the time goes in v1:
time: 163 us; the launch traced here: 162 us
  Pallas kernels  158 us (97%)
  local copies, waits for them, and re-layouts  2.87 us (2%)
    pallas_call x1, Pallas kernels, local(): pl.pallas_call(kernel, out_shape=jax.ShapeDtypeStruct((512, 768), BF16),...  158 us

profile of v1, /device:TPU:1, one launch (start us, length us, event | category | flops | bytes accessed | tf_op | source)
XLA Modules:
  0.0 162.4 jit_solution(14783886821200891215)
XLA Ops:
  0.0 0.7 pad.2.clone
  0.7 0.1 pad.3.clone
  0.8 1.4 maximum_maximum_fusion.aux_hbm
  2.2 158.1 %shard_map.82 = bf16[512,768]{1,0:T(8,128)(2,1)} custom-call(bf16[512,6144]{1,0:T(8,128)(2,1)} %x_hbm.1, bf16[192,512]{1,0:T(8,128)(2,1)} %wq_hbm.1, bf16[192,512]{1,0:T(8,128)(2,1)} %wk_hbm.1, bf16[192,512]{1,0:T(8,128)(2,1)} %wv_hbm.1, bf16[128,768]{1,0:T(8,128)(2,1)} %wo_hbm.1, f32[16,128]{1,0:T(8,128)} %maximum_maximum_fusion.aux_hbm), custom_call_target="tpu_custom_call" | custom-call | tf_op jit(solution)/shard_map/pallas_call | solution.py:460
  160.3 2.1 %copy.10 = bf16[512,768]{1,0:T(8,128)(2,1)} copy(bf16[512,768]{1,0:T(8,128)(2,1)} %shard_map.82) | data formatting | bytes 1572864
  (1 shorter events, 0.0 us)

commit v2 on v1

--- a/solution.py
+++ b/solution.py
@@ -10,8 +10,8 @@
 BF16 = jnp.bfloat16
 NZ = 8
 NY = 4
-PIECES = 2
-COPIES = 220
+COPIES = 300
+O_X = 48
 
 
 def aligned(value, by):
@@ -19,8 +19,8 @@
 
 
 def kernel(
-    x_hbm, wq_hbm, wk_hbm, wv_hbm, wo_hbm, aux_hbm, out_ref,
-    xs, wk, wv, wq, wo, acc, part, kb, vb, qb, decay, aux,
+    x_hbm, wq_hbm, wk_hbm, wv_hbm, wo_hbm, surge_ref, scale_ref, speed_ref, out_ref,
+    xs, wk, wv, wq, wo, acc, part, kb, vb, qb, decay, aux, aux_own,
     states, arrived, totals, tot_out, group_out, groups, prefix_out, prefix,
     normed, staged, oacc, ssem, rsem, lsem,
 ):
@@ -69,6 +69,12 @@
         sent.append(copy)
         return copy
 
+    aux_own[0:4, :] = surge_ref[...]
+    aux_own[4:8, :] = scale_ref[...]
+    for h in range(4):
+        aux_own[8 + h : 9 + h, :] = jnp.full((1, 128), speed_ref[h], F32)
+    aux_own[12:16, :] = jnp.zeros((4, 128), F32)
+
     barrier = pltpu.get_barrier_semaphore()
     for device in peers:
         pl.semaphore_signal(barrier, inc=1, device_id=device, device_id_type=MESH)
@@ -106,13 +112,14 @@
 
     own_piece("k", wk_hbm, wk.at[pl.ds(source_row, 192)], 0)
     own_piece("v", wv_hbm, wv.at[pl.ds(source_row, 192)], 1)
-    own_piece("aux", aux_hbm, aux, 2)
+    own_piece("aux", aux_own, aux, 2)
     half_lane = aligned(3072 * c, 128)
-    quarter = aligned(128 * y, 128)
-    x_cross = send(
-        x_hbm.at[pl.ds(quarter, 128), pl.ds(half_lane, 3072)],
-        xs.at[region, pl.ds(quarter, 128)], across_chip,
-    )
+    x_cross = []
+    for i in (0, 1):
+        some = pl.ds(aligned(128 * y + 64 * i, 64), 64)
+        x_cross.append(
+            send(x_hbm.at[some, pl.ds(half_lane, 3072)], xs.at[region, some], across_chip)
+        )
     own_piece("q", wq_hbm, wq.at[pl.ds(source_row, 192)], 3)
     x_local = pltpu.make_async_copy(x_hbm.at[:, pl.ds(half_lane, 3072)], xs.at[region], lsem.at[4])
     x_local.start()
@@ -133,10 +140,12 @@
             self.ring[f, 0, 1] = send(part, part, up)
             self.ring[f, 1, 1] = send(part, part, down)
 
-        def start(self):
+        def start_x(self):
             own = self.own_x(z)
             self.first = send(own, own, inner)
             self.begin_flow("a")
+
+        def start_z(self):
             self.begin_flow("z")
             own = self.own_z(z)
             self.side.append((0, send(own, own, inner)))
@@ -179,12 +188,93 @@
         lambda w: rows(wq, 192 * (p * NZ + w) + 96, 96, 32),
         {"a": (4, 3), "b": (3, 4), "z": (3, 4)},
     )
-    orr = Round(
-        lambda w: rows(wo, 128 * (x * NZ + w), 128, 128),
-        lambda w: rows(wo, 128 * (xi * NZ + w), 128, 128),
-        lambda w: rows(wo, 128 * (xe * NZ + w), 128, 128),
-        {"a": (4, 3), "b": (3, 4), "z": (3, 4)},
-    )
+    columns = {"x": x, "e": xe, "i": xi, "d": 3 - xi}
+
+    def o_top(f, w):
+        return rows(wo, 128 * (columns[f] * NZ + w), O_X, 16)
+
+    def o_rest(f, w):
+        return rows(wo, 128 * (columns[f] * NZ + w) + O_X, 128 - O_X, 16)
+
+    class OutRound:
+        hops = {"z": (4, 3), "x": (3, 4), "e": (4, 3), "i": (3, 4), "d": (4, 3)}
+
+        def __init__(self):
+            self.ring = {}
+            self.to_inner = {}
+            self.to_across = {}
+            self.diagonal = {}
+
+        def part(self, f, w):
+            return o_rest("x", w) if f == "z" else o_top(f, w)
+
+        def begin(self, f, source=None):
+            part = self.part(f, z)
+            source = part if source is None else source
+            self.ring[f, 0, 1] = send(source, part, up)
+            self.ring[f, 1, 1] = send(source, part, down)
+
+        def sides(self, d, way, w):
+            part = self.part("z", w)
+            self.to_inner[d, way] = send(part, part, inner)
+            self.to_across[d, way] = send(part, part, across_chip)
+
+        def early(self):
+            top, rest = wo_hbm.at[pl.ds(0, O_X)], wo_hbm.at[pl.ds(O_X, 128 - O_X)]
+            self.swap = send(top, o_top("x", z), across_chip)
+            self.begin("z", rest)
+            self.begin("x", top)
+
+        def exchange(self):
+            self.sides(0, 1, z)
+            self.tops = []
+            for f in ("x", "e"):
+                part = o_top(f, z)
+                self.tops.append(send(part, part, inner))
+
+        def start(self):
+            self.begin("e")
+            self.step(1, "zx")
+
+        def start_nbr(self):
+            for f, copy in zip(("i", "d"), self.tops):
+                copy.wait_recv()
+                self.begin(f)
+
+        def step(self, d, flows):
+            for f in flows:
+                for way in (0, 1):
+                    limit = self.hops[f][way]
+                    if d > limit:
+                        continue
+                    self.ring[f, way, d].wait_recv()
+                    w = (z + NZ - d) % NZ if way == 0 else (z + d) % NZ
+                    part = self.part(f, w)
+                    if d < limit:
+                        self.ring[f, way, d + 1] = send(part, part, up if way == 0 else down)
+                    if f == "z":
+                        self.sides(d, way, w)
+
+        def turn(self, d):
+            for way in (0, 1):
+                if (d, way) not in self.to_inner:
+                    continue
+                w = (z + NZ - d) % NZ if way == 0 else (z + d) % NZ
+                self.to_inner[d, way].wait_recv()
+                if way == 0:
+                    part = o_rest("i", w)
+                    self.diagonal[d, way] = send(part, part, across_chip)
+                self.to_across[d, way].wait_recv()
+                if way == 1:
+                    part = o_rest("e", w)
+                    self.diagonal[d, way] = send(part, part, inner)
+
+        def wait_turned(self, low, high):
+            for (d, way), copy in self.diagonal.items():
+                if low <= d <= high:
+                    copy.wait_recv()
+
+    orr = OutRound()
 
     weights = {0: wk, 1: wv, 2: wq}
     last_pair = ((z + 4) % NZ) // 2
@@ -204,9 +294,11 @@
         def _(m):
             mm_chunk(which, (last_pair + 1 + m) % 4)
 
+    orr.early()
     wait_own("k")
+    kv.start_x()
     wait_own("v")
-    kv.start()
+    kv.start_z()
     acc[...] = jnp.zeros_like(acc)
     kv.start_nbr()
     x_local.wait()
@@ -237,43 +329,49 @@
     kv.step(1)
     wait_own("q")
 
-    x_cross.wait_recv()
     theirs = 1 - region
 
     def x_rows(cy, start, count):
         return xs.at[theirs, pl.ds(aligned(128 * cy + start, 64), count)]
 
-    own_q = x_rows(y, 0, 128)
-    x_up = send(own_q, own_q, y_up)
-    x_down = send(own_q, own_q, y_down)
+    x_up, x_down = [None, None], [None, None]
+    for i in (0, 1):
+        x_cross[i].wait_recv()
+        mine = x_rows(y, 64 * i, 64)
+        x_up[i] = send(mine, mine, y_up)
+        x_down[i] = send(mine, mine, y_down)
     kv.step(2)
-    x_up.wait_recv()
+    x_up[0].wait_recv()
     far = x_rows((y + 3) % NY, 0, 64)
     x_up2 = send(far, far, y_up)
-    x_down.wait_recv()
+    x_down[1].wait_recv()
     far = x_rows((y + 1) % NY, 64, 64)
     x_down2 = send(far, far, y_down)
-    o_swap_dst = wo.at[pl.ds(o_own_row, 128)]
-    o_swap = send(wo_hbm, o_swap_dst, across_chip)
     kv.step(3)
-    qr.start()
-    x_up2.wait_recv()
-    x_down2.wait_recv()
+    qr.start_x()
+    qr.start_z()
+    for copy in (x_up[1], x_down[0], x_up2, x_down2):
+        copy.wait_recv()
     kv.wait_side(0, 3)
     qr.start_nbr()
-    mm_three((0, 1))
+    mm_chunk((0, 1), (last_pair + 1) % 4)
     kv.step(4)
+
+    @pl.loop(2, 4)
+    def _(m):
+        mm_chunk((0, 1), (last_pair + m) % 4)
+
     qr.step(1)
     kv.wait_side(4, 4)
-    mm_chunk((0, 1), last_pair)
+    mm_chunk((0,), last_pair)
     k_part = send(acc.at[0, 1 - c], part.at[0], other)
+    mm_chunk((1,), last_pair)
     v_part = send(acc.at[1, 1 - c], part.at[1], other)
-    qr.step(2)
 
     k_part.wait_recv()
-    v_part.wait_recv()
     ksum = acc[0, c] + part[0]
     kb[...] = (ksum * (1.0 / (1.0 + jnp.exp(-ksum)))).astype(BF16)
+    v_part.wait_recv()
     vb[...] = (acc[1, c] + part[1]).astype(BF16)
     for h in range(4):
         speed = aux[8 + h : 9 + h, 0:1]
@@ -289,10 +387,11 @@
     state_copies = [
         send(states.at[(z + d) % NZ], arrived.at[z], z_dev[d]) for d in range(1, NZ)
     ]
+    qr.step(2)
+    o_local.wait()
+    orr.swap.wait_recv()
+    orr.exchange()
     qr.step(3)
-    orr_ready = [False]
-    o_local.wait()
-    o_swap.wait_recv()
     orr.start()
     qr.wait_side(0, 3)
     for copy in state_copies + tot_copies:
@@ -330,104 +429,115 @@
     qr.wait_side(4, 4)
     mm_chunk((2,), last_pair)
     q_part = send(acc.at[2, 1 - c], part.at[2], other)
-    for copy in prefix_copies:
-        copy.wait_recv()
+    orr.step(1, "eid")
+    orr.step(2, "zx")
     q_part.wait_recv()
     qsum = acc[2, c] + part[2]
     qb[...] = (qsum * (1.0 / (1.0 + jnp.exp(-qsum)))).astype(BF16)
 
-    width = 512 // PIECES
+    for h in range(4):
+        cut = slice(128 * h, 128 * h + 128)
+        scores = lax.dot_general(
+            qb[:, cut], kb[:, cut], (((1,), (1,)), ((), ())), preferred_element_type=F32
+        )
+        acc[0, c, :, cut] = jnp.dot(
+            (scores * decay[h]).astype(BF16), vb[:, cut], preferred_element_type=F32
+        )
+    for copy in prefix_copies:
+        copy.wait_recv()
     swap_t = y * 2 + 1 - c
-    swap_copies = []
-    for piece in range(PIECES):
-        for h in range(piece * 4 // PIECES, (piece + 1) * 4 // PIECES):
-            cut = slice(128 * h, 128 * h + 128)
-            speed = aux[8 + h : 9 + h, 0:1]
-            q_h, k_h, v_h = qb[:, cut], kb[:, cut], vb[:, cut]
-            scores = lax.dot_general(q_h, k_h, (((1,), (1,)), ((), ())), preferred_element_type=F32)
-            inside = jnp.dot((scores * decay[h]).astype(BF16), v_h, preferred_element_type=F32)
-            carried = prefix[2 * h : 2 * h + 2].reshape(128, 128)
-            reach = jnp.exp(cs - (steps + 1.0) * speed)
-            att = inside + reach * jnp.dot(q_h, carried, preferred_element_type=F32)
-            square = jnp.mean(att * att, axis=1, keepdims=True)
-            value = (att * lax.rsqrt(square + 1e-05) * aux[4 + h : 5 + h, :]).astype(BF16)
-
-            @pl.when(home)
-            def _():
-                normed[t, :, cut] = value
-
-            @pl.when(away)
-            def _():
-                staged[:, cut] = value
-
-        lanes = pl.ds(piece * width, width)
-        copy = remote(staged.at[:, lanes], normed.at[swap_t, :, lanes], swap)
+
+    def block(cy, start, count, h):
+        return normed.at[cy * 2 + c, pl.ds(start, count), pl.ds(128 * h, 128)]
+
+    ring_up, ring_down, relays, swap_copies = [], [], [], []
+    for h in range(4):
+        cut = slice(128 * h, 128 * h + 128)
+        speed = aux[8 + h : 9 + h, 0:1]
+        carried = prefix[2 * h : 2 * h + 2].reshape(128, 128)
+        reach = jnp.exp(cs - (steps + 1.0) * speed)
+        att = acc[0, c, :, cut] + reach * jnp.dot(qb[:, cut], carried, preferred_element_type=F32)
+        square = jnp.mean(att * att, axis=1, keepdims=True)
+        value = (att * lax.rsqrt(square + 1e-05) * aux[4 + h : 5 + h, :]).astype(BF16)
+        mine = block(y, 0, 512, h)
+        ring_up.append(remote(mine, mine, y_up))
+        ring_down.append(remote(mine, mine, y_down))
+        relays.append(remote(mine, mine, other))
+        back = remote(staged.at[:, pl.ds(128 * h, 128)], normed.at[swap_t, :, pl.ds(128 * h, 128)], swap)
+        swap_copies.append(back)
+
+        @pl.when(home)
+        def _():
+            normed[t, :, cut] = value
+            ring_up[h].start()
+            ring_down[h].start()
+            relays[h].start()
 
         @pl.when(away)
         def _():
-            copy.start()
-
-        sent_away.append(copy)
-        swap_copies.append(copy)
-
-    orr.step(1)
-
-    def block(cy, start, count, piece):
-        return normed.at[cy * 2 + c, pl.ds(start, count), pl.ds(piece * width, width)]
-
-    ring_up, ring_down, relays = [], [], []
-    for piece in range(PIECES):
-        copy = swap_copies[piece]
-
-        @pl.when(away)
-        def _():
-            copy.wait_recv()
-
-        mine = block(y, 0, 512, piece)
-        ring_up.append(send(mine, mine, y_up))
-        ring_down.append(send(mine, mine, y_down))
-        relays.append(send(mine, mine, other))
-    orr.step(2)
+            staged[:, cut] = value
+            back.start()
+
+    sent.extend(ring_up + ring_down + relays)
+    sent_away.extend(swap_copies)
+    orr.step(2, "eid")
+    orr.turn(0)
+    orr.turn(1)
+    orr.step(3, "zx")
+
+    @pl.when(away)
+    def _():
+        for h in range(4):
+            swap_copies[h].wait_recv()
+            ring_up[h].start()
+            ring_down[h].start()
+            relays[h].start()
+
+    orr.turn(2)
     ring_up2, ring_down2 = [], []
-    for piece in range(PIECES):
-        ring_up[piece].wait_recv()
-        far = block((y + 3) % NY, 0, 256, piece)
+    for h in range(4):
+        ring_up[h].wait_recv()
+        far = block((y + 3) % NY, 0, 256, h)
         ring_up2.append(send(far, far, y_up))
-        whole = block((y + 3) % NY, 0, 512, piece)
+        whole = block((y + 3) % NY, 0, 512, h)
         relays.append(send(whole, whole, other))
-        ring_down[piece].wait_recv()
-        far = block((y + 1) % NY, 256, 256, piece)
+        ring_down[h].wait_recv()
+        far = block((y + 1) % NY, 256, 256, h)
         ring_down2.append(send(far, far, y_down))
-        whole = block((y + 1) % NY, 0, 512, piece)
+        whole = block((y + 1) % NY, 0, 512, h)
         relays.append(send(whole, whole, other))
+        if h == 1:
+            orr.step(3, "eid")
+            orr.step(4, "zx")
     oacc[...] = jnp.zeros_like(oacc)
-    orr.step(3)
-    for piece in range(PIECES):
-        ring_up2[piece].wait_recv()
-        far = block((y + 2) % NY, 0, 256, piece)
-        relays.append(send(far, far, other))
-        ring_down2[piece].wait_recv()
-        far = block((y + 2) % NY, 256, 256, piece)
-        relays.append(send(far, far, other))
-    orr.wait_side(0, 3)
+    orr.turn(3)
+    orr.step(4, "eid")
+    orr.turn(4)
+    last_relays = []
+    for h in range(4):
+        ring_up2[h].wait_recv()
+        far = block((y + 2) % NY, 0, 256, h)
+        last_relays.append(send(far, far, other))
+        ring_down2[h].wait_recv()
+        far = block((y + 2) % NY, 256, 256, h)
+        last_relays.append(send(far, far, other))
+    orr.wait_turned(0, 4)
     for copy in relays:
         copy.wait_recv()
 
-    def out_chunk(pair):
-        lanes = pl.ds(aligned(256 * (pair % 2), 128), 256)
-        left = jnp.concatenate([normed[2 * g + pair // 2, :, lanes] for g in range(4)], axis=1)
-        right = jnp.concatenate(
-            [wo[pl.ds(aligned(1024 * g + 256 * pair, 256), 256)] for g in range(4)], axis=0
-        )
-        return jnp.dot(left, right, preferred_element_type=F32)
-
-    @pl.loop(0, 3)
-    def _(m):
-        oacc[...] += out_chunk((last_pair + 1 + m) % 4)
-
-    orr.step(4)
-    orr.wait_side(4, 4)
-    out_ref[...] = (oacc[...] + out_chunk(last_pair)).astype(BF16)
+    def out_block(b):
+        right = wo[pl.ds(aligned(512 * b, 512), 512)]
+        return jnp.dot(normed[b], right, preferred_element_type=F32)
+
+    @pl.loop(0, 6)
+    def _(i):
+        off = i // 2 + i // 4
+        oacc[...] += out_block(((y + off) % NY) * 2 + i % 2)
+
+    for copy in last_relays:
+        copy.wait_recv()
+    b = ((y + 2) % NY) * 2
+    out_ref[...] = (oacc[...] + out_block(b) + out_block(b + 1)).astype(BF16)
 
     for copy in sent:
         copy.wait_send()
@@ -436,6 +546,7 @@
     def _():
         for copy in sent_away:
             copy.wait_send()
+    assert used[0] <= COPIES
 
 
 def local(
@@ -448,19 +559,12 @@
     channel_scaling_coefficient,
     final_projector,
 ):
-    aux = jnp.concatenate(
-        [
-            surge_fading.reshape(4, 128),
-            channel_scaling_coefficient.reshape(4, 128),
-            jnp.broadcast_to(channel_fading_speed[:, None], (4, 128)),
-            jnp.zeros((4, 128), F32),
-        ],
-        axis=0,
-    )
     return pl.pallas_call(
         kernel,
         out_shape=jax.ShapeDtypeStruct((512, 768), BF16),
-        in_specs=[pl.BlockSpec(memory_space=pl.ANY)] * 6,
+        in_specs=[pl.BlockSpec(memory_space=pl.ANY)] * 5
+        + [pl.BlockSpec(memory_space=pltpu.VMEM)] * 2
+        + [pl.BlockSpec(memory_space=pltpu.SMEM)],
         out_specs=pl.BlockSpec(memory_space=pltpu.VMEM),
         scratch_shapes=[
             pltpu.VMEM((2, 512, 3072), BF16),
@@ -474,6 +578,7 @@
             pltpu.VMEM((512, 512), BF16),
             pltpu.VMEM((512, 512), BF16),
             pltpu.VMEM((4, 512, 512), F32),
+            pltpu.VMEM((16, 128), F32),
             pltpu.VMEM((16, 128), F32),
             pltpu.VMEM((8, 64, 128), BF16),
             pltpu.VMEM((8, 64, 128), BF16),
@@ -499,7 +604,9 @@
         lookup_projector,
         content_projector,
         final_projector,
-        aux,
+        surge_fading.reshape(4, 128),
+        channel_scaling_coefficient.reshape(4, 128),
+        channel_fading_speed,
     )
 
 

time: 163 us -> 146 us (0.90)
  Pallas kernels: 158 us -> 143 us
    pallas_call x1, Pallas kernels: 158 us -> 143 us  [local(): pl.pallas_call(kernel, out_shape=jax.ShapeDtypeStruct((512, 768), BF16),...]
where the time goes in v2:
time: 146 us; the launch traced here: 145 us
  Pallas kernels  143 us (98%)
  local copies, waits for them, and re-layouts  2.06 us (1%)
    pallas_call x1, Pallas kernels, local(): pl.pallas_call(kernel, out_shape=jax.ShapeDtypeStruct((512, 768), BF16),...  143 us

profile of v2, /device:TPU:1, one launch (start us, length us, event | category | flops | bytes accessed | tf_op | source)
XLA Modules:
  0.0 145.0 jit_solution(15089681513937764755)
XLA Ops:
  0.0 142.9 %shard_map.82 = bf16[512,768]{1,0:T(8,128)(2,1)} custom-call(bf16[512,6144]{1,0:T(8,128)(2,1)} %x_hbm.1, bf16[192,512]{1,0:T(8,128)(2,1)} %wq_hbm.1, bf16[192,512]{1,0:T(8,128)(2,1)} %wk_hbm.1, bf16[192,512]{1,0:T(8,128)(2,1)} %wv_hbm.1, bf16[128,768]{1,0:T(8,128)(2,1)} %wo_hbm.1, f32[4,128]{1,0:T(4,128)} %bitcast.2, f32[4,128]{1,0:T(4,128)} %bitcast.3, ...), custom_call_target="tpu_custom_call" | custom-call | tf_op jit(solution)/shard_map/pallas_call | solution.py:562
  142.9 2.1 %copy.10 = bf16[512,768]{1,0:T(8,128)(2,1)} copy(bf16[512,768]{1,0:T(8,128)(2,1)} %shard_map.82) | data formatting | bytes 1572864

commit v3 on v2

--- a/solution.py
+++ b/solution.py
@@ -11,7 +11,7 @@
 NZ = 8
 NY = 4
 COPIES = 300
-O_X = 48
+O_X = 64
 
 
 def aligned(value, by):
@@ -483,8 +483,6 @@
     orr.step(2, "eid")
     orr.turn(0)
     orr.turn(1)
-    orr.step(3, "zx")
-
     @pl.when(away)
     def _():
         for h in range(4):
@@ -492,6 +490,8 @@
             ring_up[h].start()
             ring_down[h].start()
             relays[h].start()
+
+    orr.step(3, "zx")
 
     orr.turn(2)
     ring_up2, ring_down2 = [], []

time: 146 us -> 145 us (level)
  no operation moved by 1% of the time
where the time goes in v3:
time: 145 us
  Pallas kernels  142 us (98%)
  local copies, waits for them, and re-layouts  2.06 us (1%)
    pallas_call x1, Pallas kernels, local(): pl.pallas_call(kernel, out_shape=jax.ShapeDtypeStruct((512, 768), BF16),...  142 us

profile of v3, /device:TPU:1, one launch (start us, length us, event | category | flops | bytes accessed | tf_op | source)
XLA Modules:
  0.0 144.5 jit_solution(17284213152386247618)
XLA Ops:
  0.0 142.5 %shard_map.82 = bf16[512,768]{1,0:T(8,128)(2,1)} custom-call(bf16[512,6144]{1,0:T(8,128)(2,1)} %x_hbm.1, bf16[192,512]{1,0:T(8,128)(2,1)} %wq_hbm.1, bf16[192,512]{1,0:T(8,128)(2,1)} %wk_hbm.1, bf16[192,512]{1,0:T(8,128)(2,1)} %wv_hbm.1, bf16[128,768]{1,0:T(8,128)(2,1)} %wo_hbm.1, f32[4,128]{1,0:T(4,128)} %bitcast.2, f32[4,128]{1,0:T(4,128)} %bitcast.3, ...), custom_call_target="tpu_custom_call" | custom-call | tf_op jit(solution)/shard_map/pallas_call | solution.py:562
  142.5 2.1 %copy.10 = bf16[512,768]{1,0:T(8,128)(2,1)} copy(bf16[512,768]{1,0:T(8,128)(2,1)} %shard_map.82) | data formatting | bytes 1572864
